TPU v7x, 256 devices: a whole 4x4x8 slice. The times are simulated.
256 devices in a mesh: expert: 8 (over y, core), tensor: 32 (over z, x).
Axes of the slice: x: 4, y: 4, z: 8, core: 2. Of those that a mesh axis runs over, the one named last changes fastest.
Arguments:
- tokens: bfloat16 [2048, 6144], P('expert', 'tensor'), may hold values from -6 to 6
- expert_ids: int32 [2048, 2], P('expert'), may hold values from 0 to 7, all different within a row; in each aligned block of 256 rows (0 to 255, 256 to 511, ...) at most 96 rows name the same one
- gate_prob: float32 [2048, 2], P('expert'), may hold values from 0.1 to 1
- w_gate: bfloat16 [8, 6144, 8192], P('expert', None, 'tensor'), may hold values from -0.078125 to 0.078125
- w_up: bfloat16 [8, 6144, 8192], P('expert', None, 'tensor'), may hold values from -0.078125 to 0.078125
- w_down: bfloat16 [8, 8192, 6144], P('expert', 'tensor'), may hold values from -0.125 to 0.125
Outputs:
- mixed: bfloat16 [2048, 6144], P('expert', 'tensor')
Inputs may be any that keep to these rules, and one draw needn't show every extreme that they name: `expert_ids`: the two experts of a row differ. Within the rows of one index of expert (aligned blocks of 256 rows) no expert is named by more than 96 rows, and in every draw some expert is named by exactly 96 rows of some block.
All inputs are finite; a program needn't handle non-finite values.
Results may differ from a plain program's by a relative error of at most 0.017.
Values may be sent and summed in bfloat16 or wider, within the bound.
No kernel may reach another device: no remote copies, remote signals or barrier semaphores. Data moves between devices by JAX's collectives and lax.ppermute only.
A program may use at most 64 MiB of HBM per device.

v0:
```python
import jax
import jax.numpy as jnp
from jax import lax
from jax.sharding import PartitionSpec as P


def slot_table(ids, experts, cap):
    flat = ids.reshape(-1)
    onehot = (flat[:, None] == jnp.arange(experts, dtype=jnp.int32)[None, :]).astype(jnp.int32)
    before = jnp.cumsum(onehot, axis=0) - onehot
    position = jnp.sum(before * onehot, axis=1)
    slot = flat * cap + position
    match = slot[None, :] == jnp.arange(experts * cap, dtype=jnp.int32)[:, None]
    which = jnp.arange(flat.shape[0], dtype=jnp.int32) // 2
    owner = jnp.max(jnp.where(match, which[None, :], -1), axis=1)
    return (slot, owner)


def fill_slots(block, owner):
    picked = jnp.take(block, jnp.maximum(owner, 0), axis=0)
    return jnp.where((owner >= 0)[:, None], picked, jnp.zeros_like(picked))


def local(tokens, expert_ids, gate_prob, w_gate, w_up, w_down):
    experts = lax.axis_size("expert")
    group_rows = tokens.shape[0]
    cap = 3 * group_rows // experts
    slot, owner = slot_table(expert_ids, experts, cap)
    gate_mat = w_gate[0]
    up_mat = w_up[0]
    down_mat = w_down[0]
    columns = tokens.shape[1]
    sending = fill_slots(tokens, owner).reshape(experts, cap, columns)
    arrived = lax.all_to_all(sending, "expert", split_axis=0, concat_axis=0, tiled=True).reshape(
        experts * cap, columns
    )
    piece = lax.all_gather(arrived, "tensor", axis=1, tiled=True)
    gate = jnp.dot(piece, gate_mat, preferred_element_type=jnp.float32)
    up = jnp.dot(piece, up_mat, preferred_element_type=jnp.float32)
    hidden = (jax.nn.silu(gate) * up).astype(jnp.bfloat16)
    partial_out = jnp.dot(hidden, down_mat, preferred_element_type=jnp.float32)
    summed = lax.psum_scatter(
        partial_out.astype(jnp.bfloat16), "tensor", scatter_dimension=1, tiled=True
    ).astype(jnp.float32)
    columns = summed.shape[1]
    returned = lax.all_to_all(
        summed.reshape(experts, cap, columns).astype(jnp.bfloat16),
        "expert",
        split_axis=0,
        concat_axis=0,
        tiled=True,
    ).astype(jnp.float32)
    table = returned.reshape(experts * cap, columns)
    picked = jnp.take(table, slot, axis=0).reshape(group_rows, 2, columns)
    mixed = jnp.sum(gate_prob[:, :, None] * picked, axis=1)
    return mixed.astype(jnp.bfloat16)


def solution(mesh):
    return jax.shard_map(
        local,
        mesh=mesh,
        in_specs=(
            P("expert", "tensor"),
            P("expert", None),
            P("expert", None),
            P("expert", None, "tensor"),
            P("expert", None, "tensor"),
            P("expert", "tensor", None),
        ),
        out_specs=P("expert", "tensor"),
        check_vma=False,
    )
```

profile of v0, /device:TPU:1, one launch (start us, length us, event | category | flops | bytes accessed | tf_op | source)
XLA Modules:
  0.0 413.5 jit_solution(16867759176059031204)
XLA Ops:
  6.5 1.0 copy.36
  7.8 1.1 reduce-window.6
  9.8 1.0 copy.40
  10.8 3.3 gather_fusion
  14.1 1.3 select_select_fusion
  15.4 13.8 %all_to_all.10 = bf16[8,96,192]{2,1,0:T(8,128)(2,1)S(1)} all-to-all(bf16[8,96,192]{2,1,0:T(8,128)(2,1)S(1)} %select_select_fusion), channel_id=1, replica_groups=mesh['expert'=8,'tensor'=32] {'expert'}, dimensions={0} | all-to-all | bytes 589824 | tf_op jit(solution)/shard_map/all_to_all | solution.py:34
  29.2 0.9 copy.46
  30.1 103.6 %all-gather.2.cloned.1.call-done = bf16[768,6144]{0,1:T(8,128)(2,1)} async-done(((bf16[768,192]{0,1:T(8,128)(2,1)}), bf16[768,6144]{0,1:T(8,128)(2,1)}) %all-gather.2.cloned.1.call-update) | async-done | bytes 9437200 | tf_op jit(solution)/shard_map/all_gather | solution.py:37
  133.7 6.3 %fusion.3 = f32[768,256]{1,0:T(8,128)S(1)} fusion(bf16[768,6144]{0,1:T(8,128)(2,1)} %all-gather.2.cloned.1.call-done, bf16[1,6144,256]{2,1,0:T(8,128)(2,1)} %param.9), kind=kOutput, calls=%fused_computation.6 | convolution fusion | flops 2415919104 | bytes 13369344 | tf_op jit(solution)/shard_map/dot_general | solution.py:38
  140.1 1.0 copy-done.1
  141.1 0.9 copy-done.6
  142.0 2.7 fusion.8
  144.6 5.1 %convolution_convert_fusion = bf16[768,6144]{0,1:T(8,128)(2,1)} fusion(bf16[768,256]{1,0:T(8,128)(2,1)S(1)} %fusion.8, bf16[1,256,6144]{2,1,0:T(8,128)(2,1)S(1)} %copy-done), kind=kOutput, calls=%fused_computation.2 | convolution fusion | flops 2420637696 | bytes 12976128 | tf_op jit(solution)/shard_map/dot_general | solution.py:41
  150.8 0.8 copy.39
  151.6 0.8 copy.35
  152.4 225.5 %reduce-scatter.2.cloned.1.call-done = bf16[768,192]{0,1:T(8,128)(2,1)} async-done(((bf16[768,6144]{0,1:T(8,128)(2,1)}), bf16[768,192]{0,1:T(8,128)(2,1)}) %reduce-scatter.2.cloned.1.call-update) | async-done | bytes 294928 | tf_op jit(solution)/shard_map/reduce_scatter | solution.py:42
  377.9 1.4 convert_element_type.26
  379.3 0.8 copy.42
  380.1 9.0 %all-to-all-start.1 = ((bf16[8,96,192]{1,2,0:T(8,128)(2,1)}), bf16[8,96,192]{1,2,0:T(8,128)(2,1)S(1)}, u32[]{:S(2)}, u32[]{:S(2)}) async-start(bf16[8,96,192]{1,2,0:T(8,128)(2,1)} %copy.42), calls=%async_computation.2 | async-start | bytes 786432 | tf_op jit(solution)/shard_map/all_to_all | solution.py:46
  389.2 7.7 %all-to-all-done.1 = bf16[8,96,192]{1,2,0:T(8,128)(2,1)S(1)} async-done(((bf16[8,96,192]{1,2,0:T(8,128)(2,1)}), bf16[8,96,192]{1,2,0:T(8,128)(2,1)S(1)}, u32[]{:S(2)}, u32[]{:S(2)}) %all-to-all-start.1) | async-done | bytes 294944 | tf_op jit(solution)/shard_map/all_to_all | solution.py:46
  396.8 1.1 copy.43
  397.9 3.4 gather_fusion.1
  401.3 2.1 gather.15
  403.5 2.4 multiply_reduce_fusion
  (39 shorter events, 3.0 us)
Async XLA Ops:
  6.5 138.1 %copy-start = (bf16[1,256,6144]{2,1,0:T(8,128)(2,1)S(1)}, bf16[1,256,6144]{2,1,0:T(8,128)(2,1)}, u32[]{:S(2)}) copy-start(bf16[1,256,6144]{2,1,0:T(8,128)(2,1)} %param.11) | copy-start | bytes 9437188
  6.5 127.2 %all-gather.2.cloned.1.call-start = ((), (), s32[]{:S(2)}) async-start(), calls=%async_computation.3 | async-start | bytes 9732096 | tf_op jit(solution)/shard_map/all_gather | solution.py:37
  30.1 347.9 %reduce-scatter.2.cloned.1.call-start = ((), (), s32[]{:S(2)}) async-start(), calls=%async_computation.4 | async-start | bytes 9732096 | tf_op jit(solution)/shard_map/reduce_scatter | solution.py:42
  133.7 7.3 %copy-start.1 = (bf16[768,6144]{0,1:T(8,128)(2,1)S(1)}, bf16[768,6144]{0,1:T(8,128)(2,1)}, u32[]{:S(2)}) copy-start(bf16[768,6144]{0,1:T(8,128)(2,1)} %all-gather.2.cloned.1.call-done) | copy-start | bytes 28311556
  133.7 8.2 %copy-start.6 = (bf16[1,6144,256]{2,1,0:T(8,128)(2,1)S(1)}, bf16[1,6144,256]{2,1,0:T(8,128)(2,1)}, u32[]{:S(2)}) copy-start(bf16[1,6144,256]{2,1,0:T(8,128)(2,1)} %param.10) | copy-start | bytes 9437188
  149.7 0.7 copy-start.4
  149.7 1.9 copy-start.5
  380.1 16.7 %all-to-all-start.1 = ((bf16[8,96,192]{1,2,0:T(8,128)(2,1)}), bf16[8,96,192]{1,2,0:T(8,128)(2,1)S(1)}, u32[]{:S(2)}, u32[]{:S(2)}) async-start(bf16[8,96,192]{1,2,0:T(8,128)(2,1)} %copy.42), calls=%async_computation.2 | async-start | bytes 786432 | tf_op jit(solution)/shard_map/all_to_all | solution.py:46
  397.9 5.6 %copy-start.2 = (f32[256,2]{1,0:T(8,128)S(1)}, f32[256,2]{1,0:T(8,128)}, u32[]{:S(2)}) copy-start(f32[256,2]{1,0:T(8,128)} %copy.35) | copy-start | bytes 6148
  397.9 5.6 %copy-start.3 = (pred[256,2]{1,0:T(8,128)(4,1)S(1)}, pred[256,2]{1,0:T(8,128)(4,1)}, u32[]{:S(2)}) copy-start(pred[256,2]{1,0:T(8,128)(4,1)} %copy.39) | copy-start | bytes 1540
Sparse Core Ops, SparseCore 0:
  30.2 103.4 all-gather.1
  149.9 228.0 reduce-scatter.1
where the time goes:
time: 414 us
  waiting for transfers between devices  337 us (81%)
  local copies, waits for them, and re-layouts  20.9 us (5%)
  matrix products  14.1 us (3%)
  blocking collectives  13.8 us (3%)
  between operations  13.6 us (3%)
  starting transfers between devices  9.05 us (2%)
  other arithmetic  5.31 us (1%)
    reduce_scatter x1, waiting for transfers between devices, local(): lax.psum_scatter(partial_out.astype(jnp.bfloat16), 'tensor', scatter_dime...  226 us
    all_gather x1, waiting for transfers between devices, local(): piece = lax.all_gather(arrived, 'tensor', axis=1, tiled=True)  104 us
    all_to_all x1, blocking collectives, local(): lax.all_to_all(sending, 'expert', split_axis=0, concat_axis=0, tiled=True)  13.8 us
    all_to_all x1, starting transfers between devices, local(): lax.all_to_all(summed.reshape(experts, cap, columns).astype(jnp.bfloat16)...  9 us
  transfers between devices with their start and end apart: 3, of which 3 were waited for; matrix products, arithmetic and copies ran while one was open for 1% of the time, Pallas kernels for 0%

commit v1 on v0

--- a/solution.py
+++ b/solution.py
@@ -1,7 +1,18 @@
+import functools
 import jax
 import jax.numpy as jnp
 from jax import lax
 from jax.sharding import PartitionSpec as P
+
+
+def show_map(q_in, a_name):
+    latest = tuple((q_in for _ in range(lax.axis_size(a_name))))
+    side_arr = jnp.stack(latest)
+    tall = lax.all_to_all(side_arr, a_name, 0, 0)
+    return jnp.concatenate(tall, axis=1)
+
+
+supply_all_the_lane = functools.partial(show_map, a_name="tensor")
 
 
 def slot_table(ids, experts, cap):
@@ -34,7 +45,7 @@
     arrived = lax.all_to_all(sending, "expert", split_axis=0, concat_axis=0, tiled=True).reshape(
         experts * cap, columns
     )
-    piece = lax.all_gather(arrived, "tensor", axis=1, tiled=True)
+    piece = supply_all_the_lane(arrived)
     gate = jnp.dot(piece, gate_mat, preferred_element_type=jnp.float32)
     up = jnp.dot(piece, up_mat, preferred_element_type=jnp.float32)
     hidden = (jax.nn.silu(gate) * up).astype(jnp.bfloat16)

time: 414 us -> 524 us (1.27)
  blocking collectives: 13.8 us -> 231 us
  waiting for transfers between devices: 337 us -> 233 us
    all_to_all x0 -> x1, blocking collectives: none -> 217 us  [show_map(): tall = lax.all_to_all(side_arr, a_name, 0, 0)]
    all_gather x1 -> x0, waiting for transfers between devices: 104 us -> none  [local(): piece = lax.all_gather(arrived, 'tensor', axis=1, tiled=True)]
  transfers between devices with their start and end apart: 3 -> 2, of which waited for: 3 -> 2; matrix products, arithmetic and copies ran while one was open for 1% -> 0% of each run, Pallas kernels for 0% -> 0%
where the time goes in v1:
time: 524 us; the launch traced here: 523 us
  waiting for transfers between devices  233 us (44%)
  blocking collectives  231 us (44%)
  local copies, waits for them, and re-layouts  21 us (4%)
  between operations  13.6 us (3%)
  matrix products  10.4 us (2%)
  starting transfers between devices  9 us (2%)
  other arithmetic  5.31 us (1%)
    reduce_scatter x1, waiting for transfers between devices, local(): lax.psum_scatter(partial_out.astype(jnp.bfloat16), 'tensor', scatter_dime...  225 us
    all_to_all x1, blocking collectives, show_map(): tall = lax.all_to_all(side_arr, a_name, 0, 0)  217 us
    all_to_all x1, blocking collectives, local(): lax.all_to_all(sending, 'expert', split_axis=0, concat_axis=0, tiled=True)  13.8 us
  transfers between devices with their start and end apart: 2, of which 2 were waited for; matrix products, arithmetic and copies ran while one was open for 0% of the time, Pallas kernels for 0%

profile of v1, /device:TPU:1, one launch (start us, length us, event | category | flops | bytes accessed | tf_op | source)
XLA Modules:
  0.0 523.1 jit_solution(12169938692920097005)
XLA Ops:
  6.5 1.0 copy.37
  7.8 1.1 reduce-window.6
  9.8 1.0 copy.41
  10.8 3.3 gather_fusion
  14.1 1.3 select_select_fusion
  15.4 13.8 %all_to_all.15 = bf16[8,96,192]{2,1,0:T(8,128)(2,1)S(1)} all-to-all(bf16[8,96,192]{2,1,0:T(8,128)(2,1)S(1)} %select_select_fusion), channel_id=1, replica_groups=mesh['expert'=8,'tensor'=32] {'expert'}, dimensions={0} | all-to-all | bytes 589824 | tf_op jit(solution)/shard_map/all_to_all | solution.py:45
  29.2 0.9 copy.42
  30.0 2.0 stack.3
  32.1 217.0 %all_to_all.16 = bf16[32,768,192]{1,2,0:T(8,128)(2,1)S(1)} all-to-all(bf16[32,768,192]{1,2,0:T(8,128)(2,1)S(1)} %stack.3), channel_id=1, replica_groups=mesh['expert'=8,'tensor'=32] {'tensor'}, dimensions={0} | all-to-all | bytes 18874368 | tf_op jit(solution)/shard_map/all_to_all | solution.py:11
  249.1 2.6 fusion.3
  251.7 2.7 fusion.8
  254.4 5.1 convolution_convert_fusion
  260.6 0.8 copy.40
  261.3 0.8 copy.36
  262.1 225.4 %reduce-scatter.2.cloned.1.call-done = bf16[768,192]{0,1:T(8,128)(2,1)} async-done(((bf16[768,6144]{0,1:T(8,128)(2,1)}), bf16[768,192]{0,1:T(8,128)(2,1)}) %reduce-scatter.2.cloned.1.call-update) | async-done | bytes 294928 | tf_op jit(solution)/shard_map/reduce_scatter | solution.py:53
  487.5 1.4 convert_element_type.26
  488.9 0.8 copy.43
  489.7 9.0 %all-to-all-start.2 = ((bf16[8,96,192]{1,2,0:T(8,128)(2,1)}), bf16[8,96,192]{1,2,0:T(8,128)(2,1)S(1)}, u32[]{:S(2)}, u32[]{:S(2)}) async-start(bf16[8,96,192]{1,2,0:T(8,128)(2,1)} %copy.43), calls=%async_computation.3 | async-start | bytes 786432 | tf_op jit(solution)/shard_map/all_to_all | solution.py:57
  498.8 7.7 %all-to-all-done.2 = bf16[8,96,192]{1,2,0:T(8,128)(2,1)S(1)} async-done(((bf16[8,96,192]{1,2,0:T(8,128)(2,1)}), bf16[8,96,192]{1,2,0:T(8,128)(2,1)S(1)}, u32[]{:S(2)}, u32[]{:S(2)}) %all-to-all-start.2) | async-done | bytes 294944 | tf_op jit(solution)/shard_map/all_to_all | solution.py:57
  506.4 1.1 copy.44
  507.5 3.4 gather_fusion.1
  510.9 2.1 gather.15
  513.1 2.4 multiply_reduce_fusion
  515.5 0.7 copy.46
  (38 shorter events, 2.2 us)
Async XLA Ops:
  6.5 247.8 %copy-start = (bf16[1,256,6144]{2,1,0:T(8,128)(2,1)S(1)}, bf16[1,256,6144]{2,1,0:T(8,128)(2,1)}, u32[]{:S(2)}) copy-start(bf16[1,256,6144]{2,1,0:T(8,128)(2,1)} %param.11) | copy-start | bytes 9437188
  6.5 481.0 %reduce-scatter.2.cloned.1.call-start = ((), (), s32[]{:S(2)}) async-start(), calls=%async_computation.4 | async-start | bytes 9732096 | tf_op jit(solution)/shard_map/reduce_scatter | solution.py:53
  32.1 217.0 %copy-start.1 = (bf16[1,6144,256]{2,1,0:T(8,128)(2,1)S(1)}, bf16[1,6144,256]{2,1,0:T(8,128)(2,1)}, u32[]{:S(2)}) copy-start(bf16[1,6144,256]{2,1,0:T(8,128)(2,1)} %param.9) | copy-start | bytes 9437188
  249.1 2.6 copy-start.6
  259.5 0.7 copy-start.4
  259.5 1.9 copy-start.5
  489.7 16.7 %all-to-all-start.2 = ((bf16[8,96,192]{1,2,0:T(8,128)(2,1)}), bf16[8,96,192]{1,2,0:T(8,128)(2,1)S(1)}, u32[]{:S(2)}, u32[]{:S(2)}) async-start(bf16[8,96,192]{1,2,0:T(8,128)(2,1)} %copy.43), calls=%async_computation.3 | async-start | bytes 786432 | tf_op jit(solution)/shard_map/all_to_all | solution.py:57
  507.5 5.6 %copy-start.2 = (f32[256,2]{1,0:T(8,128)S(1)}, f32[256,2]{1,0:T(8,128)}, u32[]{:S(2)}) copy-start(f32[256,2]{1,0:T(8,128)} %copy.36) | copy-start | bytes 6148
  507.5 5.6 %copy-start.3 = (pred[256,2]{1,0:T(8,128)(4,1)S(1)}, pred[256,2]{1,0:T(8,128)(4,1)}, u32[]{:S(2)}) copy-start(pred[256,2]{1,0:T(8,128)(4,1)} %copy.40) | copy-start | bytes 1540
Sparse Core Ops, SparseCore 0:
  259.6 227.8 reduce-scatter.1
